TPU v7x, 32 devices: a whole 2x2x4 slice. The times are simulated.
32 devices in a mesh: heads: 4 (over y, core), seq: 8 (over z, x).
Axes of the slice: x: 2, y: 2, z: 4, core: 2. Of those that a mesh axis runs over, the one named last changes fastest.
Arguments:
- queries: bfloat16 [1024, 64, 576], P('seq', 'heads'), may hold values from -6 to 6
- latents: bfloat16 [8, 128, 576], P('seq', 'heads'), may hold values from -6 to 6
- grad_out: bfloat16 [1024, 64, 512], P('seq', 'heads'), may hold values from -6 to 6
- selected: int32 [8, 4], P('seq'), may hold values from 0 to 7, as said below
Outputs:
- output: bfloat16 [1024, 64, 512], P('seq', 'heads')
- grad_query: bfloat16 [1024, 64, 576], P('seq', 'heads')
- latent_grad: float32 [8, 128, 576], P('seq', 'heads')
Inputs may be any that keep to these rules, and one draw needn't show every extreme that they name: `selected`: row i lists 4 different blocks, none of them held on the same index of seq as block i (blocks i and j share it when i // 1 equals j // 1); how often a block is chosen varies widely between blocks.
All inputs are finite; a program needn't handle non-finite values.
Results may differ from a plain program's by a relative error of at most 0.012.
Values may be sent and summed in bfloat16 or wider, within the bound.
A program may use at most 64 MiB of HBM per device.

v0:
```python
import jax
import jax.numpy as jnp
from jax import lax
from jax.sharding import PartitionSpec as P


def shards(queries, latents, grad_out, selected):
    block_count, row_share, key_width = latents.shape
    token_total, head_count, _ = queries.shape
    value_width = grad_out.shape[2]
    key_blocks = selected.shape[1] + 1
    block_size = token_total // block_count
    score_scale = key_width ** (-0.5)
    slices = lax.all_gather(latents, "seq", axis=0, tiled=True)
    list_blocks = slices.shape[0]
    own_blocks = lax.axis_index("seq") * block_count + jnp.arange(block_count, dtype=jnp.int32)
    block_ids = jnp.concatenate([own_blocks[:, None], selected], axis=1).reshape(-1)
    picked = jnp.take(slices, block_ids, axis=0)
    key_row_tiles = lax.all_gather(picked, "heads", axis=1, tiled=True)
    key_row_tiles = key_row_tiles.reshape(block_count, key_blocks * block_size, key_width)
    value_rows = key_row_tiles[:, :, :value_width]
    query_row_tiles = queries.reshape(block_count, block_size, head_count, key_width)
    grad_rows = grad_out.reshape(block_count, block_size, head_count, value_width)
    scores = (
        jnp.einsum(
            "gonv,gmv->gnom", query_row_tiles, key_row_tiles, preferred_element_type=jnp.float32
        )
        * score_scale
    )
    prob_full = jax.nn.softmax(scores, axis=-1)
    prob_half = prob_full.astype(jnp.bfloat16)
    output = jnp.einsum(
        "bhtk,bkl->bthl", prob_half, value_rows, preferred_element_type=jnp.float32
    ).astype(jnp.bfloat16)
    row_delta = jnp.sum(grad_rows.astype(jnp.float32) * output.astype(jnp.float32), axis=-1)
    grad_prob = jnp.einsum(
        "bthl,bkl->bhtk", grad_rows, value_rows, preferred_element_type=jnp.float32
    )
    score_gradient = (
        prob_full * (grad_prob - jnp.transpose(row_delta, (0, 2, 1))[..., None]) * score_scale
    ).astype(jnp.bfloat16)
    grad_query = jnp.einsum(
        "mfgv,mvq->mgfq", score_gradient, key_row_tiles, preferred_element_type=jnp.float32
    ).astype(jnp.bfloat16)
    key_gradient = jnp.einsum(
        "jxnq,jnxa->jqa", score_gradient, query_row_tiles, preferred_element_type=jnp.float32
    )
    grad_value = jnp.einsum(
        "bhtk,bthl->bkl", prob_half, grad_rows, preferred_element_type=jnp.float32
    )
    key_gradient = jnp.concatenate(
        [key_gradient[:, :, :value_width] + grad_value, key_gradient[:, :, value_width:]], axis=-1
    )
    contrib = key_gradient.reshape(block_count * key_blocks, block_size, key_width)
    head_total = lax.psum(contrib, "heads")
    own_share = lax.dynamic_slice_in_dim(
        head_total, lax.axis_index("heads") * row_share, row_share, 1
    )
    one_hot = (jnp.arange(list_blocks, dtype=jnp.int32)[:, None] == block_ids[None, :]).astype(
        jnp.float32
    )
    dense_grad = jnp.dot(
        one_hot,
        own_share.reshape(block_count * key_blocks, row_share * key_width),
        precision=lax.Precision.HIGHEST,
        preferred_element_type=jnp.float32,
    )
    dense_grad = dense_grad.reshape(list_blocks, row_share, key_width)
    holders = list_blocks // block_count
    bundles = dense_grad.reshape(1, holders * block_count, row_share, key_width)
    arrived = lax.all_to_all(bundles, "seq", split_axis=1, concat_axis=0, tiled=True)
    latent_grad = jnp.sum(arrived, axis=0)
    return (
        output.reshape(token_total, head_count, value_width),
        grad_query.reshape(token_total, head_count, key_width),
        latent_grad,
    )


def solution(mesh):
    in_specs = (
        P("seq", "heads", None),
        P("seq", "heads", None),
        P("seq", "heads", None),
        P("seq", None),
    )
    out_specs = (P("seq", "heads", None), P("seq", "heads", None), P("seq", "heads", None))
    return jax.shard_map(shards, mesh=mesh, in_specs=in_specs, out_specs=out_specs, check_vma=False)
```

profile of v0, /device:TPU:0, one launch (start us, length us, event | category | flops | bytes accessed | tf_op | source)
XLA Modules:
  0.0 150.2 jit_solution(12962128840217296627)
XLA Ops:
  7.2 0.0 copy-start
  7.2 0.0 all-reduce.2.cloned.1.call-start
  7.2 0.9 compare_and_fusion
  8.1 32.9 %all_gather.6 = bf16[8,32,576]{2,1,0:T(8,128)(2,1)S(1)} all-gather(bf16[1,32,576]{2,1,0:T(8,128)(2,1)} %param.5), channel_id=1, replica_groups=mesh['heads'=4,'seq'=8] {'seq'}, dimensions={0}, use_global_device_ids=true | all-gather | bytes 331776 | tf_op jit(solution)/shard_map/all_gather | solution.py:14
  41.0 0.6 gather_fusion
  41.6 0.1 broadcast_select_fusion
  41.7 8.8 %all_gather.7 = bf16[5,128,576]{2,1,0:T(8,128)(2,1)S(1)} all-gather(bf16[5,32,576]{2,1,0:T(8,128)(2,1)S(1)} %broadcast_select_fusion), channel_id=1, replica_groups=mesh['heads'=4,'seq'=8] {'heads'}, dimensions={1}, use_global_device_ids=true | all-gather | bytes 921600 | tf_op jit(solution)/shard_map/all_gather | solution.py:19
  50.5 0.0 copy-start.2
  50.5 4.8 %copy.37 = bf16[128,16,512]{0,2,1:T(8,128)(2,1)} copy(bf16[128,16,512]{2,1,0:T(8,128)(2,1)} %param.6) | data formatting | bytes 4194304 | tf_op args[2]
  55.3 0.0 copy-done
  55.3 2.2 %bitcast_reduce_fusion = (f32[16,128]{1,0:T(8,128)S(1)}, f32[640,128,16]{1,0,2:T(8,128)S(1)}) fusion(bf16[640,576,1]{1,0,2:T(8,128)(2,1)S(1)} %bitcast.124, bf16[128,16,576]{0,2,1:T(8,128)(2,1)S(1)} %copy-done), kind=kOutput, calls=%fused_computation.6 | convolution fusion | flops 1512568832 | bytes 8347648 | tf_op jit(solution)/shard_map/gonv,gmv->gnom/dot_general | solution.py:25
  57.5 0.0 copy-start.1
  57.5 0.9 fusion.5
  58.4 0.7 copy-done.1
  59.1 3.5 %fusion.6 = (f32[128,16]{0,1:T(8,128)S(1)}, bf16[512,16,128]{2,0,1:T(8,128)(2,1)}) fusion(bf16[128,16,512]{0,2,1:T(8,128)(2,1)S(1)} %copy-done.1, f32[16,128]{1,0:T(8,128)S(1)} %fusion.5, f32[16,128]{1,0:T(8,128)S(1)} %get-tuple-element.14, f32[640,128,16]{1,0,2:T(8,128)S(1)} %get-tuple-element.15, bf16[1,640,576]{2,1,0:T(8,128)(2,1)S(1)} %bitcast.125), kind=kOutput, calls=%fused_computation.11 | convolution fusion | flops 1352660992 | bytes 10117120 | tf_op jit(solution)/shard_map/bhtk,bkl->bthl/dot_general | solution.py:32
  62.6 0.0 copy-done.2
  62.6 2.0 %fusion.7 = bf16[16,128,640]{1,2,0:T(8,128)(2,1)S(1)} fusion(f32[16,128]{1,0:T(8,128)S(1)} %bitcast.130, f32[16,128]{1,0:T(8,128)S(1)} %fusion.5, f32[16,128]{1,0:T(8,128)S(1)} %get-tuple-element.14, f32[640,128,16]{1,0,2:T(8,128)S(1)} %get-tuple-element.15, bf16[128,16,512]{0,2,1:T(8,128)(2,1)S(1)} %copy-done.1, bf16[1,640,576]{2,1,0:T(8,128)(2,1)S(1)} %bitcast.126), kind=kOutput, calls=%fused_computation.12 | convolution fusion | flops 1351352320 | bytes 10641408 | tf_op jit(solution)/shard_map/bthl,bkl->bhtk/dot_general | solution.py:36
  64.6 0.0 copy-start.3
  64.6 2.0 %convolution_bitcast_fusion = f32[1,640,576]{1,2,0:T(8,128)S(1)} fusion(bf16[16,128,640]{1,2,0:T(8,128)(2,1)S(1)} %fusion.7, bf16[128,16,576]{0,2,1:T(8,128)(2,1)S(1)} %copy-done), kind=kOutput, calls=%fused_computation.21 | convolution fusion | flops 1509949440 | bytes 6455296 | tf_op jit(solution)/shard_map/jxnq,jnxa->jqa/dot_general | solution.py:45
  66.6 0.0 copy-done.3
  66.6 1.9 %fusion.19 = f32[1,640,512]{1,2,0:T(8,128)S(1)} fusion(bf16[128,16,512]{0,2,1:T(8,128)(2,1)S(1)} %copy-done.1, f32[1,640,576]{1,2,0:T(8,128)S(1)} %convolution_bitcast_fusion, f32[16,128]{1,0:T(8,128)S(1)} %fusion.5, f32[16,128]{1,0:T(8,128)S(1)} %get-tuple-element.14, f32[640,128,16]{1,0,2:T(8,128)S(1)} %get-tuple-element.15), kind=kOutput, calls=%fused_computation.23 | convolution fusion | flops 1347747840 | bytes 9977856 | tf_op jit(solution)/shard_map/bhtk,bthl->bkl/dot_general | solution.py:48
  68.6 1.2 pad_maximum_fusion
  69.8 3.0 %copy.43 = f32[1,640,576]{2,1,0:T(8,128)} copy(f32[1,640,576]{1,2,0:T(8,128)} %pad_maximum_fusion) | data formatting | bytes 2949120 | tf_op jit(solution)/shard_map/concatenate | solution.py:51
  72.8 0.0 all-reduce.2.cloned.1.call-update
  72.8 44.1 %all-reduce.2.cloned.1.call-done = f32[5,128,576]{2,1,0:T(8,128)} async-done(((f32[5,128,576]{2,1,0:T(8,128)}), f32[5,128,576]{2,1,0:T(8,128)}) %all-reduce.2.cloned.1.call-update) | async-done | bytes 1474576 | tf_op jit(solution)/shard_map/psum | solution.py:55
  117.0 1.0 constant_dynamic-slice_fusion
  118.0 0.2 reshape.186
  118.2 0.2 dot_general.43
  118.4 0.7 convolution_bitcast_fusion.1
  119.1 1.0 copy.45
  120.0 5.5 %all-to-all-start = ((f32[1,8,32,576]{3,2,0,1:T(8,128)}), f32[1,8,32,576]{3,2,0,1:T(8,128)S(1)}, u32[]{:S(2)}, u32[]{:S(2)}) async-start(f32[1,8,32,576]{3,2,0,1:T(8,128)} %copy.45), calls=%async_computation | async-start | bytes 1310720 | tf_op jit(solution)/shard_map/all_to_all | solution.py:71
  125.5 4.5 %copy.46 = bf16[128,16,512]{2,1,0:T(8,128)(2,1)} copy(bf16[128,16,512]{0,2,1:T(8,128)(2,1)} %bitcast.123) | data formatting | bytes 4194304
  130.1 5.4 %convert_bitcast_fusion = bf16[128,16,576]{0,2,1:T(8,128)(2,1)} fusion(bf16[640,576,1]{1,0,2:T(8,128)(2,1)} %bitcast.127, bf16[16,128,640]{1,2,0:T(8,128)(2,1)} %copy-done.3), kind=kOutput, calls=%fused_computation.18 | convolution fusion | flops 1511129088 | bytes 5718016 | tf_op jit(solution)/shard_map/mfgv,mvq->mgfq/dot_general | solution.py:42
  135.5 7.2 %all-to-all-done = f32[1,8,32,576]{3,2,0,1:T(8,128)S(1)} async-done(((f32[1,8,32,576]{3,2,0,1:T(8,128)}), f32[1,8,32,576]{3,2,0,1:T(8,128)S(1)}, u32[]{:S(2)}, u32[]{:S(2)}) %all-to-all-start) | async-done | bytes 589856 | tf_op jit(solution)/shard_map/all_to_all | solution.py:71
  142.7 0.7 reduce_sum.34
  (3 shorter events, 0.0 us)
Async XLA Ops:
  7.2 48.1 %copy-start = (bf16[128,16,576]{0,2,1:T(8,128)(2,1)S(1)}, bf16[128,16,576]{0,2,1:T(8,128)(2,1)}, u32[]{:S(2)}) copy-start(bf16[128,16,576]{0,2,1:T(8,128)(2,1)} %param.4) | copy-start | bytes 7077892
  7.2 109.8 %all-reduce.2.cloned.1.call-start = ((), (), s32[]{:S(2)}) async-start(), calls=%async_computation.1 | async-start | bytes 3276800 | tf_op jit(solution)/shard_map/psum | solution.py:55
  50.5 12.1 %copy-start.2 = (bf16[5,128,576]{2,1,0:T(8,128)(2,1)}, bf16[5,128,576]{2,1,0:T(8,128)(2,1)S(1)}, u32[]{:S(2)}) copy-start(bf16[5,128,576]{2,1,0:T(8,128)(2,1)S(1)} %all_gather.7) | copy-start | bytes 2211844
  57.5 1.6 %copy-start.1 = (bf16[128,16,512]{0,2,1:T(8,128)(2,1)S(1)}, bf16[128,16,512]{0,2,1:T(8,128)(2,1)}, u32[]{:S(2)}) copy-start(bf16[128,16,512]{0,2,1:T(8,128)(2,1)} %copy.37) | copy-start | bytes 6291460
  64.6 2.0 %copy-start.3 = (bf16[16,128,640]{1,2,0:T(8,128)(2,1)}, bf16[16,128,640]{1,2,0:T(8,128)(2,1)S(1)}, u32[]{:S(2)}) copy-start(bf16[16,128,640]{1,2,0:T(8,128)(2,1)S(1)} %fusion.7) | copy-start | bytes 7864324
  120.0 22.7 %all-to-all-start = ((f32[1,8,32,576]{3,2,0,1:T(8,128)}), f32[1,8,32,576]{3,2,0,1:T(8,128)S(1)}, u32[]{:S(2)}, u32[]{:S(2)}) async-start(f32[1,8,32,576]{3,2,0,1:T(8,128)} %copy.45), calls=%async_computation | async-start | bytes 1310720 | tf_op jit(solution)/shard_map/all_to_all | solution.py:71
Sparse Core Ops, SparseCore 0:
  73.0 43.9 all-reduce.1
where the time goes:
time: 151 us; the launch traced here: 150 us
  waiting for transfers between devices  51.3 us (34%)
  blocking collectives  41.7 us (28%)
  matrix products  17.7 us (12%)
  local copies, waits for them, and re-layouts  16.1 us (11%)
  between operations  14.1 us (9%)
  starting transfers between devices  5.55 us (4%)
  other arithmetic  3.74 us (2%)
    psum x1, waiting for transfers between devices, shards(): head_total = lax.psum(contrib, 'heads')  44.1 us
    all_gather x1, blocking collectives, shards(): slices = lax.all_gather(latents, 'seq', axis=0, tiled=True)  32.9 us
    unnamed x10, local copies, waits for them, and re-layouts  10 us
    all_gather x1, blocking collectives, shards(): key_row_tiles = lax.all_gather(picked, 'heads', axis=1, tiled=True)  8.8 us
    all_to_all x1, waiting for transfers between devices, shards(): lax.all_to_all(bundles, 'seq', split_axis=1, concat_axis=0, tiled=True)  7.21 us
    all_to_all x1, starting transfers between devices, shards(): lax.all_to_all(bundles, 'seq', split_axis=1, concat_axis=0, tiled=True)  5.51 us
    dot_general x1, matrix products, shards(): jnp.einsum('mfgv,mvq->mgfq', score_gradient, key_row_tiles, preferred_ele...  5.43 us
    dot_general x1, matrix products, shards(): jnp.einsum('bhtk,bkl->bthl', prob_half, value_rows, preferred_element_typ...  3.47 us
  transfers between devices with their start and end apart: 2, of which 2 were waited for; matrix products, arithmetic and copies ran while one was open for 7% of the time, Pallas kernels for 0%

commit v1 on v0

--- a/solution.py
+++ b/solution.py
@@ -68,7 +68,9 @@
     dense_grad = dense_grad.reshape(list_blocks, row_share, key_width)
     holders = list_blocks // block_count
     bundles = dense_grad.reshape(1, holders * block_count, row_share, key_width)
-    arrived = lax.all_to_all(bundles, "seq", split_axis=1, concat_axis=0, tiled=True)
+    arrived = jnp.concatenate(
+        lax.all_to_all(jnp.stack(jnp.split(bundles, lax.axis_size("seq"), 1), 0), "seq", 0, 0), 0
+    )
     latent_grad = jnp.sum(arrived, axis=0)
     return (
         output.reshape(token_total, head_count, value_width),

time: 151 us -> 156 us (1.033)
  local copies, waits for them, and re-layouts: 16.1 us -> 20.7 us
    unnamed x10 -> x17, local copies, waits for them, and re-layouts: 10 us -> 14.9 us
  transfers between devices with their start and end apart: 2 -> 2, of which waited for: 2 -> 2; matrix products, arithmetic and copies ran while one was open for 7% -> 6% of each run, Pallas kernels for 0% -> 0%
where the time goes in v1:
time: 156 us; the launch traced here: 155 us
  waiting for transfers between devices  51.4 us (33%)
  blocking collectives  41.7 us (27%)
  local copies, waits for them, and re-layouts  20.7 us (13%)
  matrix products  17.7 us (11%)
  between operations  14.2 us (9%)
  starting transfers between devices  5.55 us (4%)
  other arithmetic  4.35 us (3%)
    psum x1, waiting for transfers between devices, shards(): head_total = lax.psum(contrib, 'heads')  44.1 us
    all_gather x1, blocking collectives, shards(): slices = lax.all_gather(latents, 'seq', axis=0, tiled=True)  32.9 us
    unnamed x17, local copies, waits for them, and re-layouts  14.9 us
    all_gather x1, blocking collectives, shards(): key_row_tiles = lax.all_gather(picked, 'heads', axis=1, tiled=True)  8.8 us
    all_to_all x1, waiting for transfers between devices, shards(): lax.all_to_all(jnp.stack(jnp.split(bundles, lax.axis_size('seq'), 1), 0),...  7.21 us
    all_to_all x1, starting transfers between devices, shards(): lax.all_to_all(jnp.stack(jnp.split(bundles, lax.axis_size('seq'), 1), 0),...  5.51 us
    dot_general x1, matrix products, shards(): jnp.einsum('mfgv,mvq->mgfq', score_gradient, key_row_tiles, preferred_ele...  5.43 us
    dot_general x1, matrix products, shards(): jnp.einsum('bhtk,bkl->bthl', prob_half, value_rows, preferred_element_typ...  3.47 us
  transfers between devices with their start and end apart: 2, of which 2 were waited for; matrix products, arithmetic and copies ran while one was open for 6% of the time, Pallas kernels for 0%

profile of v1, /device:TPU:0, one launch (start us, length us, event | category | flops | bytes accessed | tf_op | source)
XLA Modules:
  0.0 155.4 jit_solution(11803299763647799855)
XLA Ops:
  7.2 0.0 copy-start
  7.2 0.0 all-reduce.2.cloned.1.call-start
  7.2 0.9 compare_and_fusion
  8.1 32.9 %all_gather.6 = bf16[8,32,576]{2,1,0:T(8,128)(2,1)S(1)} all-gather(bf16[1,32,576]{2,1,0:T(8,128)(2,1)} %param.5), channel_id=1, replica_groups=mesh['heads'=4,'seq'=8] {'seq'}, dimensions={0}, use_global_device_ids=true | all-gather | bytes 331776 | tf_op jit(solution)/shard_map/all_gather | solution.py:14
  41.0 0.6 gather_fusion
  41.6 0.1 broadcast_select_fusion
  41.7 8.8 %all_gather.7 = bf16[5,128,576]{2,1,0:T(8,128)(2,1)S(1)} all-gather(bf16[5,32,576]{2,1,0:T(8,128)(2,1)S(1)} %broadcast_select_fusion), channel_id=1, replica_groups=mesh['heads'=4,'seq'=8] {'heads'}, dimensions={1}, use_global_device_ids=true | all-gather | bytes 921600 | tf_op jit(solution)/shard_map/all_gather | solution.py:19
  50.5 0.0 copy-start.2
  50.5 4.8 %copy.37 = bf16[128,16,512]{0,2,1:T(8,128)(2,1)} copy(bf16[128,16,512]{2,1,0:T(8,128)(2,1)} %param.6) | data formatting | bytes 4194304 | tf_op args[2]
  55.3 0.0 copy-done
  55.3 2.2 %bitcast_reduce_fusion = (f32[16,128]{1,0:T(8,128)S(1)}, f32[640,128,16]{1,0,2:T(8,128)S(1)}) fusion(bf16[640,576,1]{1,0,2:T(8,128)(2,1)S(1)} %bitcast.156, bf16[128,16,576]{0,2,1:T(8,128)(2,1)S(1)} %copy-done), kind=kOutput, calls=%fused_computation.6 | convolution fusion | flops 1512568832 | bytes 8347648 | tf_op jit(solution)/shard_map/gonv,gmv->gnom/dot_general | solution.py:25
  57.5 0.0 copy-start.1
  57.5 0.9 fusion.5
  58.4 0.7 copy-done.1
  59.1 3.5 %fusion.6 = (f32[128,16]{0,1:T(8,128)S(1)}, bf16[512,16,128]{2,0,1:T(8,128)(2,1)}) fusion(bf16[128,16,512]{0,2,1:T(8,128)(2,1)S(1)} %copy-done.1, f32[16,128]{1,0:T(8,128)S(1)} %fusion.5, f32[16,128]{1,0:T(8,128)S(1)} %get-tuple-element.14, f32[640,128,16]{1,0,2:T(8,128)S(1)} %get-tuple-element.15, bf16[1,640,576]{2,1,0:T(8,128)(2,1)S(1)} %bitcast.157), kind=kOutput, calls=%fused_computation.11 | convolution fusion | flops 1352660992 | bytes 10117120 | tf_op jit(solution)/shard_map/bhtk,bkl->bthl/dot_general | solution.py:32
  62.6 0.0 copy-done.2
  62.6 2.0 %fusion.7 = bf16[16,128,640]{1,2,0:T(8,128)(2,1)S(1)} fusion(f32[16,128]{1,0:T(8,128)S(1)} %bitcast.162, f32[16,128]{1,0:T(8,128)S(1)} %fusion.5, f32[16,128]{1,0:T(8,128)S(1)} %get-tuple-element.14, f32[640,128,16]{1,0,2:T(8,128)S(1)} %get-tuple-element.15, bf16[128,16,512]{0,2,1:T(8,128)(2,1)S(1)} %copy-done.1, bf16[1,640,576]{2,1,0:T(8,128)(2,1)S(1)} %bitcast.158), kind=kOutput, calls=%fused_computation.12 | convolution fusion | flops 1351352320 | bytes 10641408 | tf_op jit(solution)/shard_map/bthl,bkl->bhtk/dot_general | solution.py:36
  64.6 0.0 copy-start.3
  64.6 2.0 %convolution_bitcast_fusion = f32[1,640,576]{1,2,0:T(8,128)S(1)} fusion(bf16[16,128,640]{1,2,0:T(8,128)(2,1)S(1)} %fusion.7, bf16[128,16,576]{0,2,1:T(8,128)(2,1)S(1)} %copy-done), kind=kOutput, calls=%fused_computation.21 | convolution fusion | flops 1509949440 | bytes 6455296 | tf_op jit(solution)/shard_map/jxnq,jnxa->jqa/dot_general | solution.py:45
  66.6 0.0 copy-done.3
  66.6 1.9 %fusion.19 = f32[1,640,512]{1,2,0:T(8,128)S(1)} fusion(bf16[128,16,512]{0,2,1:T(8,128)(2,1)S(1)} %copy-done.1, f32[1,640,576]{1,2,0:T(8,128)S(1)} %convolution_bitcast_fusion, f32[16,128]{1,0:T(8,128)S(1)} %fusion.5, f32[16,128]{1,0:T(8,128)S(1)} %get-tuple-element.14, f32[640,128,16]{1,0,2:T(8,128)S(1)} %get-tuple-element.15), kind=kOutput, calls=%fused_computation.23 | convolution fusion | flops 1347747840 | bytes 9977856 | tf_op jit(solution)/shard_map/bhtk,bthl->bkl/dot_general | solution.py:48
  68.5 1.2 pad_maximum_fusion
  69.8 3.0 %copy.43 = f32[1,640,576]{2,1,0:T(8,128)} copy(f32[1,640,576]{1,2,0:T(8,128)} %pad_maximum_fusion) | data formatting | bytes 2949120 | tf_op jit(solution)/shard_map/concatenate | solution.py:51
  72.8 0.0 all-reduce.2.cloned.1.call-update
  72.8 44.1 %all-reduce.2.cloned.1.call-done = f32[5,128,576]{2,1,0:T(8,128)} async-done(((f32[5,128,576]{2,1,0:T(8,128)}), f32[5,128,576]{2,1,0:T(8,128)}) %all-reduce.2.cloned.1.call-update) | async-done | bytes 1474576 | tf_op jit(solution)/shard_map/psum | solution.py:55
  117.0 1.0 constant_dynamic-slice_fusion
  118.0 0.2 reshape.185
  118.2 0.2 dot_general.43
  118.4 0.7 convolution_bitcast_fusion.1
  119.1 0.7 fusion.30
  119.7 0.7 fusion.29
  120.4 0.7 fusion.28
  121.1 0.7 fusion.27
  121.8 0.7 fusion.26
  122.5 0.7 fusion.25
  123.2 0.7 fusion.24
  123.9 0.7 fusion.23
  124.6 5.5 %all-to-all-start = ((f32[8,1,1,32,576]{4,1,3,2,0:T(1,128)}), f32[8,1,1,32,576]{4,1,3,2,0:T(1,128)S(1)}, u32[]{:S(2)}, u32[]{:S(2)}) async-start(f32[8,1,1,32,576]{4,1,3,2,0:T(1,128)} %fusion.23), calls=%async_computation | async-start | bytes 1310720 | tf_op jit(solution)/shard_map/all_to_all | solution.py:72
  130.2 4.5 %copy.45 = bf16[128,16,512]{2,1,0:T(8,128)(2,1)} copy(bf16[128,16,512]{0,2,1:T(8,128)(2,1)} %bitcast.155) | data formatting | bytes 4194304
  134.7 5.4 %convert_bitcast_fusion = bf16[128,16,576]{0,2,1:T(8,128)(2,1)} fusion(bf16[640,576,1]{1,0,2:T(8,128)(2,1)} %bitcast.159, bf16[16,128,640]{1,2,0:T(8,128)(2,1)} %copy-done.3), kind=kOutput, calls=%fused_computation.18 | convolution fusion | flops 1511129088 | bytes 5718016 | tf_op jit(solution)/shard_map/mfgv,mvq->mgfq/dot_general | solution.py:42
  140.1 7.2 %all-to-all-done = f32[8,1,1,32,576]{4,1,3,2,0:T(1,128)S(1)} async-done(((f32[8,1,1,32,576]{4,1,3,2,0:T(1,128)}), f32[8,1,1,32,576]{4,1,3,2,0:T(1,128)S(1)}, u32[]{:S(2)}, u32[]{:S(2)}) %all-to-all-start) | async-done | bytes 589856 | tf_op jit(solution)/shard_map/all_to_all | solution.py:72
  147.3 1.3 reduce_sum.34
  (3 shorter events, 0.0 us)
Async XLA Ops:
  7.2 48.1 %copy-start = (bf16[128,16,576]{0,2,1:T(8,128)(2,1)S(1)}, bf16[128,16,576]{0,2,1:T(8,128)(2,1)}, u32[]{:S(2)}) copy-start(bf16[128,16,576]{0,2,1:T(8,128)(2,1)} %param.4) | copy-start | bytes 7077892
  7.2 109.8 %all-reduce.2.cloned.1.call-start = ((), (), s32[]{:S(2)}) async-start(), calls=%async_computation.1 | async-start | bytes 3276800 | tf_op jit(solution)/shard_map/psum | solution.py:55
  50.5 12.1 %copy-start.2 = (bf16[5,128,576]{2,1,0:T(8,128)(2,1)}, bf16[5,128,576]{2,1,0:T(8,128)(2,1)S(1)}, u32[]{:S(2)}) copy-start(bf16[5,128,576]{2,1,0:T(8,128)(2,1)S(1)} %all_gather.7) | copy-start | bytes 2211844
  57.5 1.6 %copy-start.1 = (bf16[128,16,512]{0,2,1:T(8,128)(2,1)S(1)}, bf16[128,16,512]{0,2,1:T(8,128)(2,1)}, u32[]{:S(2)}) copy-start(bf16[128,16,512]{0,2,1:T(8,128)(2,1)} %copy.37) | copy-start | bytes 6291460
  64.6 2.0 %copy-start.3 = (bf16[16,128,640]{1,2,0:T(8,128)(2,1)}, bf16[16,128,640]{1,2,0:T(8,128)(2,1)S(1)}, u32[]{:S(2)}) copy-start(bf16[16,128,640]{1,2,0:T(8,128)(2,1)S(1)} %fusion.7) | copy-start | bytes 7864324
  124.6 22.7 %all-to-all-start = ((f32[8,1,1,32,576]{4,1,3,2,0:T(1,128)}), f32[8,1,1,32,576]{4,1,3,2,0:T(1,128)S(1)}, u32[]{:S(2)}, u32[]{:S(2)}) async-start(f32[8,1,1,32,576]{4,1,3,2,0:T(1,128)} %fusion.23), calls=%async_computation | async-start | bytes 1310720 | tf_op jit(solution)/shard_map/all_to_all | solution.py:72
Sparse Core Ops, SparseCore 0:
  72.9 43.9 all-reduce.1
